TPU v7x, 128 devices: a whole 4x4x4 slice. The times are simulated.
128 devices in a mesh: gz: 16 (over y_lo, z, core), ta: 8 (over y_hi, x).
Axes of the slice: x: 4, y: 4 (y_hi: 2, y_lo: 2; y = y_hi * 2 + y_lo), z: 4, core: 2. Of those that a mesh axis runs over, the one named last changes fastest.
Arguments:
- charge: float32 [1024, 128, 128], P('gz', 'ta'), may hold values from -6 to 6
- green_hat: float32 [256, 256, 2048], P(None, 'ta', 'gz'), may hold values from 0.5 to 5
Outputs:
- potential: float32 [1024, 128, 128], P('gz', 'ta')
All inputs are finite; a program needn't handle non-finite values.
Results may differ from a plain program's by a relative error of at most 0.00007.
Values sent between devices are 32-bit elements; how exact they have to be, the bound alone decides.
A program may use at most 64 MiB of HBM per device.

v0:
```python
import functools

import jax
import jax.numpy as jnp
import ml_dtypes
import numpy as np
from jax import lax
from jax.experimental import pallas as pl
from jax.experimental.pallas import tpu as pltpu
from jax.sharding import PartitionSpec as P

MESH = pl.DeviceIdType.MESH
F32 = jnp.float32
BF16 = jnp.bfloat16
CHUNKS = 4
KY = 32
KY_STEP = KY // CHUNKS


def halves(table):
    high = table.astype(ml_dtypes.bfloat16)
    low = (table - high.astype(np.float64)).astype(ml_dtypes.bfloat16)
    return np.stack([high, low])


def tables():
    peer = np.arange(32)
    own = np.arange(4)
    x_of = (own[None] // 2) * 64 + (peer[:, None] // 8) * 16 + (peer[:, None] % 8) * 2 + own[None] % 2
    kx = np.arange(256)
    angle = 2 * np.pi / 256 * (kx[:, None, None] * x_of[None] % 256)
    cosine, sine = np.cos(angle), np.sin(angle)
    wx = np.stack([np.stack([cosine, sine], 2), np.stack([-sine, cosine], 2)]).reshape(512, 256)
    y = np.arange(128)
    wy = []
    for y_half in range(2):
        ky = 128 * y_half + np.arange(128)
        angle = 2 * np.pi / 256 * (ky[:, None] * y[None] % 256)
        cosine, sine = np.cos(angle), np.sin(angle)
        wy.append(np.block([[cosine, sine], [-sine, cosine]]))
    wy = np.stack(wy)
    v = np.arange(128)
    low_bits = np.concatenate([2 * np.arange(64), 2 * np.arange(64) + 1])
    angle = 2 * np.pi / 128 * (low_bits[:, None] * v[None] % 128)
    alpha = np.stack([np.cos(angle), np.sin(angle)]).astype(np.float32)
    reverse = np.array([0, 2, 1, 3])
    s = 4 * reverse[None, :, None] + 2 * np.arange(2)[:, None, None] + np.arange(2)[None, None]
    angle = 2 * np.pi / 2048 * (s.reshape(2, 8)[..., None] * v % 2048)
    beta = np.stack([np.cos(angle), np.sin(angle)], 2).astype(np.float32)
    beta = np.pad(beta, ((0, 0), (0, 0), (0, 6), (0, 0)))
    return (
        halves(wx),
        halves(wx.T * 2.0**-27),
        np.stack([halves(w) for w in wy]),
        np.stack([halves(w.T) for w in wy]),
        alpha,
        beta,
    )


def split(value):
    high = value.astype(BF16)
    return high, (value - high.astype(F32)).astype(BF16)


def weight3(high, low):
    return jnp.concatenate([high, high, low], axis=1)


def data3(value, axis):
    high, low = split(value)
    return jnp.concatenate([high, low, high], axis=axis)


def dot_nn(weight, data):
    return jnp.dot(weight, data, preferred_element_type=F32)


def dot_nt(weight, data):
    return lax.dot_general(weight, data, (((1,), (1,)), ((), ())), preferred_element_type=F32)


def kernel(
    charge, green, wx_hbm, wxi_hbm, wy_hbm, wyi_hbm, alpha_hbm, beta_hbm,
    out,
    g, wx, wxi, wy, wyi, alpha, beta, wz, wzi, zs, raw, a, send, recv, back, home, b, part, partial, total, final,
    load_sem, z_sem, z_out, y_sem, y_out, a_sem, a_out, h_sem, h_out, r_sem, r_out, f_sem, f_out, keep_sem,
):
    gz = lax.axis_index("gz")
    ta = lax.axis_index("ta")
    yl, q = gz // 8, gz % 8
    z, core = q // 2, q % 2
    yh, xc = ta // 4, ta % 4
    ym = yl * 2 + yh
    me = xc * 8 + q

    def plane(peer):
        return (yl * 8 + peer % 8, yh * 4 + peer // 8)

    def ring(member):
        return ((member // 2) * 8 + q, (member % 2) * 4 + xc)

    loads = [
        pltpu.make_async_copy(alpha_hbm, alpha, load_sem.at[0]),
        pltpu.make_async_copy(beta_hbm.at[yl], beta, load_sem.at[1]),
        pltpu.make_async_copy(wy_hbm.at[yh], wy, load_sem.at[2]),
        pltpu.make_async_copy(wx_hbm, wx, load_sem.at[3]),
        pltpu.make_async_copy(green, g, load_sem.at[4]),
        pltpu.make_async_copy(wxi_hbm, wxi, load_sem.at[5]),
        pltpu.make_async_copy(wyi_hbm.at[yh], wyi, load_sem.at[6]),
    ]
    for load in loads:
        load.start()

    barrier = pltpu.get_barrier_semaphore()

    def greet(step, carry):
        pl.semaphore_signal(barrier, inc=1, device_id=plane((me + step) % 32), device_id_type=MESH)
        return carry

    lax.fori_loop(1, 32, greet, 0)
    for step in range(1, 4):
        pl.semaphore_signal(barrier, inc=1, device_id=ring((ym + step) % 4), device_id_type=MESH)
    rows = charge.reshape(64 * 16, 128)
    for x in range(16):
        zs[x] = rows[pl.ds(x, 64, stride=16), :]
    pl.semaphore_wait(barrier, 34)

    for i in range(2):
        keep = pltpu.make_async_copy(
            zs.at[2 * q + i], raw.at[ym, i, z, pl.ds(core * 64, 64)], z_sem.at[i]
        )
        keep.start()

        def spread(step, carry):
            peer = (q + step) % 8
            pltpu.make_async_remote_copy(
                zs.at[2 * peer + i], raw.at[ym, i, z, pl.ds(core * 64, 64)], z_out, z_sem.at[i],
                device_id=(yl * 8 + peer, ta), device_id_type=MESH,
            ).start()
            return carry

        lax.fori_loop(1, 8, spread, 0)

    loads[0].wait()
    loads[1].wait()

    def build(slot, carry):
        turn = beta[slot]
        cos_b, sin_b = turn[0:1], turn[1:2]
        cos_a, sin_a = alpha[0], alpha[1]
        cosine = cos_a * cos_b - sin_a * sin_b
        sine = sin_a * cos_b + cos_a * sin_b
        blocks = []
        for k in range(2):
            c_k, s_k = cosine[k * 64 : k * 64 + 64], sine[k * 64 : k * 64 + 64]
            blocks += [jnp.concatenate([c_k, s_k], 1), jnp.concatenate([-s_k, c_k], 1)]
        table = jnp.concatenate(blocks, 0)
        high, low = split(table)
        wz[slot, 0] = high
        wz[slot, 1] = low
        odd = (slot % 2).astype(F32)
        wide = jnp.concatenate(
            [piece for block in blocks for piece in (block * (1.0 - odd), block * odd)], 0
        )
        high, low = split(wide.T)
        half = pl.multiple_of((slot % 2) * 256, 256)
        wzi[slot // 2, 0, pl.ds(half, 256), :] = high
        wzi[slot // 2, 1, pl.ds(half, 256), :] = low
        return carry

    lax.fori_loop(0, 8, build, 0)

    def ring_copy(i, step):
        return pltpu.make_async_remote_copy(
            raw.at[ym, i], raw.at[ym, i], y_out.at[i], y_sem.at[i, step - 1],
            device_id=ring((ym + step) % 4), device_id_type=MESH,
        )

    for i in range(2):
        pltpu.make_async_copy(raw.at[ym, i], raw.at[ym, i], z_sem.at[i]).wait()
        for step in (2, 1, 3):
            ring_copy(i, step).start()

    first = yl == 0
    sigma = jnp.where(first, 1.0, -1.0).astype(F32)

    def pick(zero, one):
        return jnp.where(first, np.float32(zero), np.float32(one))

    cos_t = [[pick(np.cos(np.pi * (e) * n / 8), np.cos(np.pi * (2 + e) * n / 8)) for n in range(4)] for e in range(2)]
    sin_t = [[pick(np.sin(np.pi * (e) * n / 8), np.sin(np.pi * (2 + e) * n / 8)) for n in range(4)] for e in range(2)]
    slots = (0, 2, 1, 3)

    def over_slabs(i):
        for row in range(2):

            def step(n, carry):
                at = pl.multiple_of(n * 16, 16)
                near = [raw[row, i, k, pl.ds(at, 16), :] for k in range(4)]
                far = [raw[2 + row, i, k, pl.ds(at, 16), :] for k in range(4)]
                for e in range(2):
                    re, im = [], []
                    for k in range(4):
                        ct, st = cos_t[e][k], sin_t[e][k]
                        if e == 0:
                            u = near[k] + sigma * far[k]
                            re.append(u * ct if k else u)
                            im.append(-(u * st) if k else jnp.zeros_like(u))
                        else:
                            w = sigma * far[k]
                            re.append(near[k] * ct - w * st if k else near[k])
                            im.append(-(near[k] * st + w * ct) if k else -w)
                    ar, ai = re[0] + re[2], im[0] + im[2]
                    br, bi = re[0] - re[2], im[0] - im[2]
                    cr, ci = re[1] + re[3], im[1] + im[3]
                    dr, di = re[1] - re[3], im[1] - im[3]
                    sums = [(ar + cr, ai + ci), (br + di, bi - dr), (ar - cr, ai - ci), (br - di, bi + dr)]
                    for j in range(4):
                        for c in range(2):
                            high, low = split(sums[j][c])
                            spot = pl.ds(pl.multiple_of(c * 128 + at, 16), 16)
                            a[slots[j], e, 0, spot, row * 128 : row * 128 + 128] = high
                            a[slots[j], e, 1, spot, row * 128 : row * 128 + 128] = low
                return carry

            lax.fori_loop(0, 8, step, 0)

    send_rows = send.reshape(32 * 256, 128)
    home_rows = home.reshape(32 * 256, 128)

    def forward_zy(i):
        def step(zt, carry):
            outs = []
            for e in range(2):
                weight = weight3(wz[zt * 2 + e, 0], wz[zt * 2 + e, 1])
                high, low = a[zt, e, 0], a[zt, e, 1]
                outs.append(dot_nn(weight, jnp.concatenate([high, low, high], 0)))
            for row in range(2):
                lanes = slice(row * 128, row * 128 + 128)
                field = jnp.concatenate(
                    [
                        jnp.concatenate([outs[e][k * 128 : k * 128 + 64, lanes], outs[e][k * 128 + 64 : k * 128 + 128, lanes]], 1)
                        for k in range(2)
                        for e in range(2)
                    ],
                    0,
                )
                plane_out = dot_nt(weight3(wy[0], wy[1]), data3(field, 1))
                for c in range(2):
                    for xt in range(4):
                        for k in range(2):
                            start = (xt * 8 + zt * 2 + k) * 256 + c * 4 + row * 2 + i
                            send_rows[pl.ds(start, 32, stride=8), :] = plane_out[
                                c * 128 + xt * 32 : c * 128 + xt * 32 + 32, k * 128 : k * 128 + 128
                            ]
            return carry

        lax.fori_loop(0, 4, step, 0)

    loads[2].wait()
    for i in range(2):
        for step in range(1, 4):
            ring_copy(i, step).wait_recv()
        over_slabs(i)
        forward_zy(i)

    my_rows = pl.ds(pl.multiple_of(me * 8, 8), 8)
    for chunk in range(CHUNKS):
        span = pl.ds(chunk * KY_STEP, KY_STEP)
        pltpu.make_async_copy(send.at[me, span], recv.at[span, my_rows], a_sem.at[chunk]).start()

        def exchange(step, carry):
            peer = (me + step) % 32
            pltpu.make_async_remote_copy(
                send.at[peer, span], recv.at[span, my_rows], a_out, a_sem.at[chunk],
                device_id=plane(peer), device_id_type=MESH,
            ).start()
            return carry

        lax.fori_loop(1, 32, exchange, 0)

    loads[3].wait()
    loads[4].wait()
    loads[5].wait()
    green_rows = g.reshape(256 * 32, 128)
    for chunk in range(CHUNKS):
        span = pl.ds(chunk * KY_STEP, KY_STEP)
        pltpu.make_async_copy(recv.at[span], recv.at[span], a_sem.at[chunk]).wait()

        def solve(n, carry):
            ky = chunk * KY_STEP + 2 * n
            field = jnp.concatenate([recv[ky], recv[ky + 1]], 1)
            full = dot_nn(weight3(wx[0], wx[1]), data3(field, 0))
            factor = jnp.concatenate(
                [green_rows[pl.ds(ky, 256, stride=32), :], green_rows[pl.ds(ky + 1, 256, stride=32), :]], 1
            )
            product = jnp.concatenate([full[:256] * factor, full[256:] * factor], 0)
            result = dot_nn(weight3(wxi[0], wxi[1]), data3(product, 0))
            back[ky] = result[:, :128]
            back[ky + 1] = result[:, 128:]
            return carry

        lax.fori_loop(0, KY_STEP // 2, solve, 0)
        pltpu.make_async_copy(back.at[span, my_rows], home.at[me, span], h_sem).start()

        def give_back(step, carry):
            peer = (me + step) % 32
            pltpu.make_async_remote_copy(
                back.at[span, pl.ds(pl.multiple_of(peer * 8, 8), 8)], home.at[me, span], h_out, h_sem,
                device_id=plane(peer), device_id_type=MESH,
            ).start()
            return carry

        lax.fori_loop(1, 32, give_back, 0)

    loads[6].wait()
    pltpu.make_async_copy(home, home, h_sem).wait()

    def inverse_yz(row):
        def step(zt, carry):
            pieces = []
            for i in range(2):
                columns = []
                for k in range(2):
                    blocks = []
                    for c in range(2):
                        for xt in range(4):
                            start = (xt * 8 + zt * 2 + k) * 256 + c * 4 + row * 2 + i
                            blocks.append(home_rows[pl.ds(start, 32, stride=8), :])
                    columns.append(jnp.concatenate(blocks, 0))
                along = dot_nn(weight3(wyi[0], wyi[1]), data3(jnp.concatenate(columns, 1), 0))
                pieces.append(
                    jnp.concatenate([along[c * 128 : c * 128 + 128, k * 128 : k * 128 + 128] for k in range(2) for c in range(2)], 1)
                )
            b[zt] = dot_nt(weight3(wzi[zt, 0], wzi[zt, 1]), data3(jnp.concatenate(pieces, 0), 1))
            return carry

        lax.fori_loop(0, 4, step, 0)

    def back_to_slabs(row):
        for i in range(2):
            lanes = slice(i * 128, i * 128 + 128)

            def step(n, carry):
                at = n * 8
                turned = []
                for e in range(2):
                    value = [
                        [b[slots[j], pl.ds(pl.multiple_of(e * 256 + c * 128 + at, 8), 8), lanes] for c in range(2)]
                        for j in range(4)
                    ]
                    (ar, ai), (br, bi), (cr, ci), (dr, di) = [
                        (value[l][0] + s * value[m][0], value[l][1] + s * value[m][1])
                        for l, m, s in ((0, 2, 1.0), (0, 2, -1.0), (1, 3, 1.0), (1, 3, -1.0))
                    ]
                    sums = [(ar + cr, ai + ci), (br - di, bi + dr), (ar - cr, ai - ci), (br + di, bi - dr)]
                    turned.append(
                        [
                            (re * cos_t[e][k] - im * sin_t[e][k], re * sin_t[e][k] + im * cos_t[e][k])
                            for k, (re, im) in enumerate(sums)
                        ]
                    )
                for k in range(4):
                    part[0, row, k, i, pl.ds(pl.multiple_of(at, 8), 8), :] = turned[0][k][0] + turned[1][k][0]
                    part[1, row, k, i, pl.ds(pl.multiple_of(at, 8), 8), :] = sigma * (turned[0][k][0] - turned[1][k][1])
                return carry

            lax.fori_loop(0, 16, step, 0)

    def sum_copy(member):
        return pltpu.make_async_remote_copy(
            part.at[member // 2, member % 2], partial.at[(ym - member) % 4 - 1], r_out, r_sem.at[(ym - member) % 4 - 1],
            device_id=ring(member), device_id_type=MESH,
        )

    other = 1 - yh
    inverse_yz(other)
    back_to_slabs(other)
    sum_copy(other).start()
    sum_copy(2 + other).start()
    inverse_yz(yh)
    back_to_slabs(yh)
    sum_copy((1 - yl) * 2 + yh).start()
    for step in range(3):
        pltpu.make_async_copy(partial.at[step], partial.at[step], r_sem.at[step]).wait()

    def add(n, carry):
        k, i = n // 2, n % 2
        total[k, i] = (part[yl, yh, k, i] + partial[0, k, i]) + (partial[1, k, i] + partial[2, k, i])
        return carry

    lax.fori_loop(0, 8, add, 0)
    pltpu.make_async_copy(total.at[z, :, pl.ds(core * 64, 64)], final.at[q], f_sem).start()

    def return_slab(step, carry):
        peer = (q + step) % 8
        pltpu.make_async_remote_copy(
            total.at[peer // 2, :, pl.ds((peer % 2) * 64, 64)], final.at[q], f_out, f_sem,
            device_id=(yl * 8 + peer, ta), device_id_type=MESH,
        ).start()
        return carry

    lax.fori_loop(1, 8, return_slab, 0)
    pltpu.make_async_copy(final, final, f_sem).wait()
    out_rows = out.reshape(64 * 16, 128)
    for x in range(16):
        out_rows[pl.ds(x, 64, stride=16), :] = final[x // 2, x % 2]

    def drain(ref, sem):
        pltpu.make_async_copy(ref, ref, sem).wait()

    drain(zs.at[pl.ds(0, 14)], z_out)
    for i in range(2):
        drain(raw.at[pl.ds(0, 3), i], y_out.at[i])
    drain(send.at[pl.ds(0, 31)], a_out)
    drain(send.at[pl.ds(0, 31)], h_out)
    drain(partial, r_out)
    drain(final.at[pl.ds(0, 7)], f_out)


def on_device(consts, charge, green_hat):
    any_spec = pl.BlockSpec(memory_space=pl.ANY)
    vmem_spec = pl.BlockSpec(memory_space=pltpu.VMEM)
    dma = pltpu.SemaphoreType.DMA
    return pl.pallas_call(
        kernel,
        out_shape=jax.ShapeDtypeStruct((64, 16, 128), F32),
        in_specs=[vmem_spec] + [any_spec] * 7,
        out_specs=vmem_spec,
        scratch_shapes=[
            pltpu.VMEM((256, 32, 128), F32),
            pltpu.VMEM((2, 512, 256), BF16),
            pltpu.VMEM((2, 256, 512), BF16),
            pltpu.VMEM((2, 256, 256), BF16),
            pltpu.VMEM((2, 256, 256), BF16),
            pltpu.VMEM((2, 128, 128), F32),
            pltpu.VMEM((8, 8, 128), F32),
            pltpu.VMEM((8, 2, 256, 256), BF16),
            pltpu.VMEM((4, 2, 512, 512), BF16),
            pltpu.VMEM((16, 64, 128), F32),
            pltpu.VMEM((4, 2, 4, 128, 128), F32),
            pltpu.VMEM((4, 2, 2, 256, 256), BF16),
            pltpu.VMEM((32, 32, 8, 128), F32),
            pltpu.VMEM((32, 256, 128), F32),
            pltpu.VMEM((32, 256, 128), F32),
            pltpu.VMEM((32, 32, 8, 128), F32),
            pltpu.VMEM((4, 512, 256), F32),
            pltpu.VMEM((2, 2, 4, 2, 128, 128), F32),
            pltpu.VMEM((3, 4, 2, 128, 128), F32),
            pltpu.VMEM((4, 2, 128, 128), F32),
            pltpu.VMEM((8, 2, 64, 128), F32),
            dma((7,)),
            dma((2,)),
            dma,
            dma((2, 3)),
            dma((2,)),
            dma((CHUNKS,)),
            dma,
            dma,
            dma,
            dma((3,)),
            dma,
            dma,
            dma,
            dma,
        ],
        compiler_params=pltpu.CompilerParams(
            collective_id=0, has_side_effects=True, vmem_limit_bytes=60 * 1024 * 1024
        ),
    )(charge, green_hat, *consts)


def solution(mesh):
    consts = tables()
    return jax.shard_map(
        functools.partial(on_device, consts),
        mesh=mesh,
        in_specs=(P("gz", "ta", None), P(None, "ta", "gz")),
        out_specs=P("gz", "ta", None),
        check_vma=False,
    )
```

profile of v0, /device:TPU:1, one launch (start us, length us, event | category | flops | bytes accessed | tf_op | source)
XLA Modules:
  0.0 191.7 jit_solution(16700279323608356478)
XLA Ops:
  0.0 189.9 %shard_map.82 = f32[64,16,128]{2,1,0:T(8,128)} custom-call(f32[64,16,128]{2,1,0:T(8,128)} %charge.1, f32[256,32,128]{2,1,0:T(8,128)} %green.1, bf16[2,512,256]{2,1,0:T(8,128)(2,1)} %constant.12.clone.wx_hbm, bf16[2,256,512]{2,1,0:T(8,128)(2,1)} %constant.13.clone.wxi_hbm, bf16[2,2,256,256]{3,2,1,0:T(8,128)(2,1)} %constant.14.clone.wy_hbm, ...), custom_call_target="tpu_custom_call" | custom-call | tf_op jit(solution)/shard_map/pallas_call | solution.py:426
  189.9 1.9 copy.10
where the time goes:
time: 195 us; the launch traced here: 192 us
  Pallas kernels  190 us (97%)
    pallas_call x1, Pallas kernels, on_device(): pl.pallas_call(kernel, out_shape=jax.ShapeDtypeStruct((64, 16, 128), F32)...  190 us

commit v1 on v0

--- a/solution.py
+++ b/solution.py
@@ -13,8 +13,7 @@
 F32 = jnp.float32
 BF16 = jnp.bfloat16
 CHUNKS = 4
-KY = 32
-KY_STEP = KY // CHUNKS
+PAIR_STEP = 16 // CHUNKS
 
 
 def halves(table):
@@ -25,16 +24,16 @@
 
 def tables():
     peer = np.arange(32)
-    own = np.arange(4)
-    x_of = (own[None] // 2) * 64 + (peer[:, None] // 8) * 16 + (peer[:, None] % 8) * 2 + own[None] % 2
+    pair = np.arange(2)
+    x_of = (pair * 64)[None, None] + ((peer // 8) * 16 + (peer % 8) * 2)[None, :, None] + pair[:, None, None]
     kx = np.arange(256)
-    angle = 2 * np.pi / 256 * (kx[:, None, None] * x_of[None] % 256)
+    angle = 2 * np.pi / 256 * (kx[:, None, None, None] * x_of[None] % 256)
     cosine, sine = np.cos(angle), np.sin(angle)
-    wx = np.stack([np.stack([cosine, sine], 2), np.stack([-sine, cosine], 2)]).reshape(512, 256)
+    wx = np.stack([np.stack([cosine, sine], 3), np.stack([-sine, cosine], 3)]).reshape(512, 256)
     y = np.arange(128)
     wy = []
     for y_half in range(2):
-        ky = 128 * y_half + np.arange(128)
+        ky = 128 * y_half + np.arange(128).reshape(4, 16, 2).transpose(0, 2, 1).reshape(128)
         angle = 2 * np.pi / 256 * (ky[:, None] * y[None] % 256)
         cosine, sine = np.cos(angle), np.sin(angle)
         wy.append(np.block([[cosine, sine], [-sine, cosine]]))
@@ -84,7 +83,7 @@
     charge, green, wx_hbm, wxi_hbm, wy_hbm, wyi_hbm, alpha_hbm, beta_hbm,
     out,
     g, wx, wxi, wy, wyi, alpha, beta, wz, wzi, zs, raw, a, send, recv, back, home, b, part, partial, total, final,
-    load_sem, z_sem, z_out, y_sem, y_out, a_sem, a_out, h_sem, h_out, r_sem, r_out, f_sem, f_out, keep_sem,
+    load_sem, z_sem, z_out, y_sem, y_out, a_sem, a_out, h_sem, h_out, r_sem, r_out, f_sem, f_out,
 ):
     gz = lax.axis_index("gz")
     ta = lax.axis_index("ta")
@@ -226,11 +225,41 @@
 
             lax.fori_loop(0, 8, step, 0)
 
-    send_rows = send.reshape(32 * 256, 128)
-    home_rows = home.reshape(32 * 256, 128)
+    send_rows = send.reshape(2 * 32 * 128, 128)
+    home_rows = home.reshape(2 * 32 * 128, 128)
+    my_first = pl.ds(pl.multiple_of(me * 8, 8), 8)
+    my_second = pl.ds(pl.multiple_of(256 + me * 8, 8), 8)
+
+    def partner(step):
+        turn = step // 2
+        return ((xc + turn) % 4) * 8 + ((z + turn // 4 + turn) % 4) * 2 + (core + step) % 2
+
+
+    def first_copy(peer):
+        return pltpu.make_async_remote_copy(
+            send.at[0, peer], recv.at[:, my_first], a_out.at[0], a_sem.at[CHUNKS], device_id=plane(peer), device_id_type=MESH
+        )
+
+    def send_first(zt, mine):
+        def step(n, carry):
+            peer = ((xc + n // 2) % 4) * 8 + zt * 2 + (core + n) % 2
+            keep = jnp.logical_and(mine, n == 0)
+
+            @pl.when(keep)
+            def _():
+                pltpu.make_async_copy(send.at[0, me], recv.at[:, my_first], a_sem.at[CHUNKS]).start()
+
+            @pl.when(jnp.logical_not(keep))
+            def _():
+                first_copy(peer).start()
+
+            return carry
+
+        lax.fori_loop(0, 8, step, 0)
 
     def forward_zy(i):
-        def step(zt, carry):
+        def step(n, carry):
+            zt = (z + n) % 4
             outs = []
             for e in range(2):
                 weight = weight3(wz[zt * 2 + e, 0], wz[zt * 2 + e, 1])
@@ -249,14 +278,24 @@
                 plane_out = dot_nt(weight3(wy[0], wy[1]), data3(field, 1))
                 for c in range(2):
                     for xt in range(4):
-                        for k in range(2):
-                            start = (xt * 8 + zt * 2 + k) * 256 + c * 4 + row * 2 + i
-                            send_rows[pl.ds(start, 32, stride=8), :] = plane_out[
-                                c * 128 + xt * 32 : c * 128 + xt * 32 + 32, k * 128 : k * 128 + 128
-                            ]
+                        for odd in range(2):
+                            at = c * 128 + xt * 32 + odd * 16
+                            for k in range(2):
+                                start = (i * 32 + xt * 8 + zt * 2 + k) * 128 + c * 4 + row * 2 + odd
+                                send_rows[pl.ds(start, 16, stride=8), :] = plane_out[
+                                    at : at + 16, k * 128 : k * 128 + 128
+                                ]
+            if i == 0:
+
+                @pl.when(n > 0)
+                def _():
+                    send_first((z + n - 1) % 4, n == 1)
+
             return carry
 
         lax.fori_loop(0, 4, step, 0)
+        if i == 0:
+            send_first((z + 3) % 4, False)
 
     loads[2].wait()
     for i in range(2):
@@ -265,15 +304,14 @@
         over_slabs(i)
         forward_zy(i)
 
-    my_rows = pl.ds(pl.multiple_of(me * 8, 8), 8)
     for chunk in range(CHUNKS):
-        span = pl.ds(chunk * KY_STEP, KY_STEP)
-        pltpu.make_async_copy(send.at[me, span], recv.at[span, my_rows], a_sem.at[chunk]).start()
+        span = pl.ds(chunk * PAIR_STEP, PAIR_STEP)
+        pltpu.make_async_copy(send.at[1, me, span], recv.at[span, my_second], a_sem.at[chunk]).start()
 
         def exchange(step, carry):
-            peer = (me + step) % 32
+            peer = partner(step)
             pltpu.make_async_remote_copy(
-                send.at[peer, span], recv.at[span, my_rows], a_out, a_sem.at[chunk],
+                send.at[1, peer, span], recv.at[span, my_second], a_out.at[1], a_sem.at[chunk],
                 device_id=plane(peer), device_id_type=MESH,
             ).start()
             return carry
@@ -284,50 +322,59 @@
     loads[4].wait()
     loads[5].wait()
     green_rows = g.reshape(256 * 32, 128)
+    recv_rows = recv.reshape(16 * 512, 128)
+    back_rows = back.reshape(16 * 512, 128)
+
+    def give_back(i, span):
+        mine = pl.ds(pl.multiple_of(i * 256 + me * 8, 8), 8)
+        pltpu.make_async_copy(back.at[span, mine], home.at[i, me, span], h_sem.at[i]).start()
+
+        def step(n, carry):
+            peer = partner(n)
+            pltpu.make_async_remote_copy(
+                back.at[span, pl.ds(pl.multiple_of(i * 256 + peer * 8, 8), 8)], home.at[i, me, span],
+                h_out.at[i], h_sem.at[i], device_id=plane(peer), device_id_type=MESH,
+            ).start()
+            return carry
+
+        lax.fori_loop(1, 32, step, 0)
+
+    whole = recv.at[:, pl.ds(0, 256)]
+    pltpu.make_async_copy(whole, whole, a_sem.at[CHUNKS]).wait()
     for chunk in range(CHUNKS):
-        span = pl.ds(chunk * KY_STEP, KY_STEP)
-        pltpu.make_async_copy(recv.at[span], recv.at[span], a_sem.at[chunk]).wait()
+        span = pl.ds(chunk * PAIR_STEP, PAIR_STEP)
+        arrived = recv.at[span, pl.ds(256, 256)]
+        pltpu.make_async_copy(arrived, arrived, a_sem.at[chunk]).wait()
 
         def solve(n, carry):
-            ky = chunk * KY_STEP + 2 * n
-            field = jnp.concatenate([recv[ky], recv[ky + 1]], 1)
+            pair = chunk * PAIR_STEP + n
+            field = jnp.concatenate([recv_rows[pl.ds(pair * 512 + odd, 256, stride=2), :] for odd in range(2)], 1)
             full = dot_nn(weight3(wx[0], wx[1]), data3(field, 0))
-            factor = jnp.concatenate(
-                [green_rows[pl.ds(ky, 256, stride=32), :], green_rows[pl.ds(ky + 1, 256, stride=32), :]], 1
-            )
+            factor = jnp.concatenate([green_rows[pl.ds(2 * pair + odd, 256, stride=32), :] for odd in range(2)], 1)
             product = jnp.concatenate([full[:256] * factor, full[256:] * factor], 0)
             result = dot_nn(weight3(wxi[0], wxi[1]), data3(product, 0))
-            back[ky] = result[:, :128]
-            back[ky + 1] = result[:, 128:]
-            return carry
-
-        lax.fori_loop(0, KY_STEP // 2, solve, 0)
-        pltpu.make_async_copy(back.at[span, my_rows], home.at[me, span], h_sem).start()
-
-        def give_back(step, carry):
-            peer = (me + step) % 32
-            pltpu.make_async_remote_copy(
-                back.at[span, pl.ds(pl.multiple_of(peer * 8, 8), 8)], home.at[me, span], h_out, h_sem,
-                device_id=plane(peer), device_id_type=MESH,
-            ).start()
-            return carry
-
-        lax.fori_loop(1, 32, give_back, 0)
+            for odd in range(2):
+                back_rows[pl.ds(pair * 512 + odd, 256, stride=2), :] = result[:, odd * 128 : odd * 128 + 128]
+            return carry
+
+        lax.fori_loop(0, PAIR_STEP, solve, 0)
+        give_back(0, span)
+    give_back(1, pl.ds(0, 16))
 
     loads[6].wait()
-    pltpu.make_async_copy(home, home, h_sem).wait()
-
-    def inverse_yz(row):
+
+    def inverse_yz(i):
         def step(zt, carry):
             pieces = []
-            for i in range(2):
+            for row in range(2):
                 columns = []
                 for k in range(2):
                     blocks = []
                     for c in range(2):
                         for xt in range(4):
-                            start = (xt * 8 + zt * 2 + k) * 256 + c * 4 + row * 2 + i
-                            blocks.append(home_rows[pl.ds(start, 32, stride=8), :])
+                            for odd in range(2):
+                                start = (i * 32 + xt * 8 + zt * 2 + k) * 128 + c * 4 + row * 2 + odd
+                                blocks.append(home_rows[pl.ds(start, 16, stride=8), :])
                     columns.append(jnp.concatenate(blocks, 0))
                 along = dot_nn(weight3(wyi[0], wyi[1]), data3(jnp.concatenate(columns, 1), 0))
                 pieces.append(
@@ -338,9 +385,8 @@
 
         lax.fori_loop(0, 4, step, 0)
 
-    def back_to_slabs(row):
-        for i in range(2):
-            lanes = slice(i * 128, i * 128 + 128)
+    def back_to_slabs(i, row):
+        for lanes in (pl.ds(pl.multiple_of(row * 128, 128), 128),):
 
             def step(n, carry):
                 at = n * 8
@@ -362,50 +408,60 @@
                         ]
                     )
                 for k in range(4):
-                    part[0, row, k, i, pl.ds(pl.multiple_of(at, 8), 8), :] = turned[0][k][0] + turned[1][k][0]
-                    part[1, row, k, i, pl.ds(pl.multiple_of(at, 8), 8), :] = sigma * (turned[0][k][0] - turned[1][k][1])
+                    part[0, row, i, k, pl.ds(pl.multiple_of(at, 8), 8), :] = turned[0][k][0] + turned[1][k][0]
+                    part[1, row, i, k, pl.ds(pl.multiple_of(at, 8), 8), :] = sigma * (turned[0][k][0] - turned[1][k][1])
                 return carry
 
             lax.fori_loop(0, 16, step, 0)
 
-    def sum_copy(member):
+    def sum_copy(i, member):
+        slot = (ym - member) % 4 - 1
         return pltpu.make_async_remote_copy(
-            part.at[member // 2, member % 2], partial.at[(ym - member) % 4 - 1], r_out, r_sem.at[(ym - member) % 4 - 1],
+            part.at[member // 2, member % 2, i], partial.at[slot, i], r_out.at[i], r_sem.at[i, slot],
             device_id=ring(member), device_id_type=MESH,
         )
 
     other = 1 - yh
-    inverse_yz(other)
-    back_to_slabs(other)
-    sum_copy(other).start()
-    sum_copy(2 + other).start()
-    inverse_yz(yh)
-    back_to_slabs(yh)
-    sum_copy((1 - yl) * 2 + yh).start()
-    for step in range(3):
-        pltpu.make_async_copy(partial.at[step], partial.at[step], r_sem.at[step]).wait()
-
-    def add(n, carry):
-        k, i = n // 2, n % 2
-        total[k, i] = (part[yl, yh, k, i] + partial[0, k, i]) + (partial[1, k, i] + partial[2, k, i])
-        return carry
-
-    lax.fori_loop(0, 8, add, 0)
-    pltpu.make_async_copy(total.at[z, :, pl.ds(core * 64, 64)], final.at[q], f_sem).start()
-
-    def return_slab(step, carry):
-        peer = (q + step) % 8
-        pltpu.make_async_remote_copy(
-            total.at[peer // 2, :, pl.ds((peer % 2) * 64, 64)], final.at[q], f_out, f_sem,
-            device_id=(yl * 8 + peer, ta), device_id_type=MESH,
-        ).start()
-        return carry
-
-    lax.fori_loop(1, 8, return_slab, 0)
-    pltpu.make_async_copy(final, final, f_sem).wait()
+
+    def home_half(i):
+        pltpu.make_async_copy(home.at[i], home.at[i], h_sem.at[i]).wait()
+        inverse_yz(i)
+        back_to_slabs(i, other)
+        sum_copy(i, other).start()
+        sum_copy(i, 2 + other).start()
+        back_to_slabs(i, yh)
+        sum_copy(i, (1 - yl) * 2 + yh).start()
+
+    def finish(i):
+        for step in range(3):
+            pltpu.make_async_copy(partial.at[step, i], partial.at[step, i], r_sem.at[i, step]).wait()
+
+        def add(k, carry):
+            total[k, i] = (part[yl, yh, i, k] + partial[0, i, k]) + (partial[1, i, k] + partial[2, i, k])
+            return carry
+
+        lax.fori_loop(0, 4, add, 0)
+        pltpu.make_async_copy(total.at[z, i, pl.ds(core * 64, 64)], final.at[q, i], f_sem.at[i]).start()
+
+        def return_slab(step, carry):
+            peer = (q + step) % 8
+            pltpu.make_async_remote_copy(
+                total.at[peer // 2, i, pl.ds((peer % 2) * 64, 64)], final.at[q, i], f_out.at[i], f_sem.at[i],
+                device_id=(yl * 8 + peer, ta), device_id_type=MESH,
+            ).start()
+            return carry
+
+        lax.fori_loop(1, 8, return_slab, 0)
+
+    home_half(0)
+    finish(0)
+    home_half(1)
+    finish(1)
     out_rows = out.reshape(64 * 16, 128)
-    for x in range(16):
-        out_rows[pl.ds(x, 64, stride=16), :] = final[x // 2, x % 2]
+    for i in range(2):
+        pltpu.make_async_copy(final.at[:, i], final.at[:, i], f_sem.at[i]).wait()
+        for n in range(8):
+            out_rows[pl.ds(2 * n + i, 64, stride=16), :] = final[n, i]
 
     def drain(ref, sem):
         pltpu.make_async_copy(ref, ref, sem).wait()
@@ -413,10 +469,11 @@
     drain(zs.at[pl.ds(0, 14)], z_out)
     for i in range(2):
         drain(raw.at[pl.ds(0, 3), i], y_out.at[i])
-    drain(send.at[pl.ds(0, 31)], a_out)
-    drain(send.at[pl.ds(0, 31)], h_out)
-    drain(partial, r_out)
-    drain(final.at[pl.ds(0, 7)], f_out)
+    for i in range(2):
+        drain(send.at[i, pl.ds(0, 31)], a_out.at[i])
+        drain(send.at[i, pl.ds(0, 31)], h_out.at[i])
+        drain(partial.at[:, i], r_out.at[i])
+        drain(final.at[pl.ds(0, 7), i], f_out.at[i])
 
 
 def on_device(consts, charge, green_hat):
@@ -441,13 +498,13 @@
             pltpu.VMEM((16, 64, 128), F32),
             pltpu.VMEM((4, 2, 4, 128, 128), F32),
             pltpu.VMEM((4, 2, 2, 256, 256), BF16),
-            pltpu.VMEM((32, 32, 8, 128), F32),
-            pltpu.VMEM((32, 256, 128), F32),
-            pltpu.VMEM((32, 256, 128), F32),
-            pltpu.VMEM((32, 32, 8, 128), F32),
+            pltpu.VMEM((2, 32, 16, 8, 128), F32),
+            pltpu.VMEM((16, 512, 128), F32),
+            pltpu.VMEM((16, 512, 128), F32),
+            pltpu.VMEM((2, 32, 16, 8, 128), F32),
             pltpu.VMEM((4, 512, 256), F32),
-            pltpu.VMEM((2, 2, 4, 2, 128, 128), F32),
-            pltpu.VMEM((3, 4, 2, 128, 128), F32),
+            pltpu.VMEM((2, 2, 2, 4, 128, 128), F32),
+            pltpu.VMEM((3, 2, 4, 128, 128), F32),
             pltpu.VMEM((4, 2, 128, 128), F32),
             pltpu.VMEM((8, 2, 64, 128), F32),
             dma((7,)),
@@ -455,15 +512,14 @@
             dma,
             dma((2, 3)),
             dma((2,)),
-            dma((CHUNKS,)),
-            dma,
-            dma,
-            dma,
-            dma((3,)),
-            dma,
-            dma,
-            dma,
-            dma,
+            dma((CHUNKS + 1,)),
+            dma((2,)),
+            dma((2,)),
+            dma((2,)),
+            dma((2, 3)),
+            dma((2,)),
+            dma((2,)),
+            dma((2,)),
         ],
         compiler_params=pltpu.CompilerParams(
             collective_id=0, has_side_effects=True, vmem_limit_bytes=60 * 1024 * 1024

time: 195 us -> 165 us (0.85)
  Pallas kernels: 190 us -> 161 us
    pallas_call x1, Pallas kernels: 190 us -> 161 us  [on_device(): pl.pallas_call(kernel, out_shape=jax.ShapeDtypeStruct((64, 16, 128), F32)...]
where the time goes in v1:
time: 165 us; the launch traced here: 163 us
  Pallas kernels  161 us (98%)
  local copies, waits for them, and re-layouts  1.87 us (1%)
    pallas_call x1, Pallas kernels, on_device(): pl.pallas_call(kernel, out_shape=jax.ShapeDtypeStruct((64, 16, 128), F32)...  161 us

profile of v1, /device:TPU:1, one launch (start us, length us, event | category | flops | bytes accessed | tf_op | source)
XLA Modules:
  0.0 163.2 jit_solution(5192210538098198876)
XLA Ops:
  0.0 161.3 %shard_map.82 = f32[64,16,128]{2,1,0:T(8,128)} custom-call(f32[64,16,128]{2,1,0:T(8,128)} %charge.1, f32[256,32,128]{2,1,0:T(8,128)} %green.1, bf16[2,512,256]{2,1,0:T(8,128)(2,1)} %constant.12.clone.wx_hbm, bf16[2,256,512]{2,1,0:T(8,128)(2,1)} %constant.13.clone.wxi_hbm, bf16[2,2,256,256]{3,2,1,0:T(8,128)(2,1)} %constant.14.clone.wy_hbm, ...), custom_call_target="tpu_custom_call" | custom-call | tf_op jit(solution)/shard_map/pallas_call | solution.py:483
  161.3 1.9 %copy.10 = f32[64,16,128]{2,1,0:T(8,128)} copy(f32[64,16,128]{2,1,0:T(8,128)} %shard_map.82) | data formatting | bytes 1048576

commit v2 on v1

--- a/solution.py
+++ b/solution.py
@@ -13,7 +13,7 @@
 F32 = jnp.float32
 BF16 = jnp.bfloat16
 CHUNKS = 4
-PAIR_STEP = 16 // CHUNKS
+QUADS = 8 // CHUNKS
 
 
 def halves(table):
@@ -24,16 +24,16 @@
 
 def tables():
     peer = np.arange(32)
-    pair = np.arange(2)
-    x_of = (pair * 64)[None, None] + ((peer // 8) * 16 + (peer % 8) * 2)[None, :, None] + pair[:, None, None]
+    row = np.arange(4)
+    x_of = ((peer // 8) * 16 + (peer % 8) * 2)[None, :] + ((row // 2) * 64 + row % 2)[:, None]
     kx = np.arange(256)
-    angle = 2 * np.pi / 256 * (kx[:, None, None, None] * x_of[None] % 256)
+    angle = 2 * np.pi / 256 * (kx[:, None, None] * x_of[None] % 256)
     cosine, sine = np.cos(angle), np.sin(angle)
     wx = np.stack([np.stack([cosine, sine], 3), np.stack([-sine, cosine], 3)]).reshape(512, 256)
     y = np.arange(128)
     wy = []
     for y_half in range(2):
-        ky = 128 * y_half + np.arange(128).reshape(4, 16, 2).transpose(0, 2, 1).reshape(128)
+        ky = 128 * y_half + np.arange(128).reshape(4, 8, 4).transpose(0, 2, 1).reshape(128)
         angle = 2 * np.pi / 256 * (ky[:, None] * y[None] % 256)
         cosine, sine = np.cos(angle), np.sin(angle)
         wy.append(np.block([[cosine, sine], [-sine, cosine]]))
@@ -178,7 +178,9 @@
 
     for i in range(2):
         pltpu.make_async_copy(raw.at[ym, i], raw.at[ym, i], z_sem.at[i]).wait()
-        for step in (2, 1, 3):
+        ring_copy(i, 2).start()
+    for i in range(2):
+        for step in (1, 3):
             ring_copy(i, step).start()
 
     first = yl == 0
@@ -191,8 +193,8 @@
     sin_t = [[pick(np.sin(np.pi * (e) * n / 8), np.sin(np.pi * (2 + e) * n / 8)) for n in range(4)] for e in range(2)]
     slots = (0, 2, 1, 3)
 
-    def over_slabs(i):
-        for row in range(2):
+    def over_slabs(row, i):
+        for _ in range(1):
 
             def step(n, carry):
                 at = pl.multiple_of(n * 16, 16)
@@ -219,181 +221,186 @@
                         for c in range(2):
                             high, low = split(sums[j][c])
                             spot = pl.ds(pl.multiple_of(c * 128 + at, 16), 16)
-                            a[slots[j], e, 0, spot, row * 128 : row * 128 + 128] = high
-                            a[slots[j], e, 1, spot, row * 128 : row * 128 + 128] = low
+                            a[slots[j], e, 0, spot, :] = high
+                            a[slots[j], e, 1, spot, :] = low
                 return carry
 
             lax.fori_loop(0, 8, step, 0)
 
-    send_rows = send.reshape(2 * 32 * 128, 128)
-    home_rows = home.reshape(2 * 32 * 128, 128)
-    my_first = pl.ds(pl.multiple_of(me * 8, 8), 8)
-    my_second = pl.ds(pl.multiple_of(256 + me * 8, 8), 8)
+    send_rows = send.reshape(4 * 32 * 64, 128)
+    home_rows = home.reshape(32 * 256, 128)
+    mine = pl.ds(pl.multiple_of(me * 8, 8), 8)
 
     def partner(step):
         turn = step // 2
         return ((xc + turn) % 4) * 8 + ((z + turn // 4 + turn) % 4) * 2 + (core + step) % 2
 
 
-    def first_copy(peer):
+    def plane_copy(line, peer, span, slot, sem):
         return pltpu.make_async_remote_copy(
-            send.at[0, peer], recv.at[:, my_first], a_out.at[0], a_sem.at[CHUNKS], device_id=plane(peer), device_id_type=MESH
+            send.at[line, peer, span], recv.at[span, line, mine], a_out.at[slot], sem,
+            device_id=plane(peer), device_id_type=MESH,
         )
 
-    def send_first(zt, mine):
+    def plane_keep(line, span, sem):
+        pltpu.make_async_copy(send.at[line, me, span], recv.at[span, line, mine], sem).start()
+
+    def send_first(line, zt, here):
         def step(n, carry):
             peer = ((xc + n // 2) % 4) * 8 + zt * 2 + (core + n) % 2
-            keep = jnp.logical_and(mine, n == 0)
+            keep = jnp.logical_and(here, n == 0)
 
             @pl.when(keep)
             def _():
-                pltpu.make_async_copy(send.at[0, me], recv.at[:, my_first], a_sem.at[CHUNKS]).start()
+                plane_keep(line, pl.ds(0, 8), a_sem.at[0])
 
             @pl.when(jnp.logical_not(keep))
             def _():
-                first_copy(peer).start()
+                plane_copy(line, peer, pl.ds(0, 8), 0, a_sem.at[0]).start()
 
             return carry
 
         lax.fori_loop(0, 8, step, 0)
 
-    def forward_zy(i):
+    def send_line(order, line, span, sem):
+        plane_keep(line, span, sem)
+
         def step(n, carry):
-            zt = (z + n) % 4
+            plane_copy(line, partner(n), span, order, sem).start()
+            return carry
+
+        lax.fori_loop(1, 32, step, 0)
+
+    def far_first(n):
+        return (z + jnp.where(n == 0, 2, jnp.where(n == 1, 1, jnp.where(n == 2, 3, 0)))) % 4
+
+    def forward_zy(order, line):
+        def step(n, carry):
+            zt = far_first(n)
             outs = []
             for e in range(2):
                 weight = weight3(wz[zt * 2 + e, 0], wz[zt * 2 + e, 1])
                 high, low = a[zt, e, 0], a[zt, e, 1]
                 outs.append(dot_nn(weight, jnp.concatenate([high, low, high], 0)))
-            for row in range(2):
-                lanes = slice(row * 128, row * 128 + 128)
-                field = jnp.concatenate(
-                    [
-                        jnp.concatenate([outs[e][k * 128 : k * 128 + 64, lanes], outs[e][k * 128 + 64 : k * 128 + 128, lanes]], 1)
-                        for k in range(2)
-                        for e in range(2)
-                    ],
-                    0,
-                )
-                plane_out = dot_nt(weight3(wy[0], wy[1]), data3(field, 1))
-                for c in range(2):
-                    for xt in range(4):
-                        for odd in range(2):
-                            at = c * 128 + xt * 32 + odd * 16
-                            for k in range(2):
-                                start = (i * 32 + xt * 8 + zt * 2 + k) * 128 + c * 4 + row * 2 + odd
-                                send_rows[pl.ds(start, 16, stride=8), :] = plane_out[
-                                    at : at + 16, k * 128 : k * 128 + 128
-                                ]
-            if i == 0:
+            field = jnp.concatenate(
+                [
+                    jnp.concatenate([outs[e][k * 128 : k * 128 + 64], outs[e][k * 128 + 64 : k * 128 + 128]], 1)
+                    for k in range(2)
+                    for e in range(2)
+                ],
+                0,
+            )
+            plane_out = dot_nt(weight3(wy[0], wy[1]), data3(field, 1))
+            for c in range(2):
+                for xt in range(4):
+                    for r in range(4):
+                        at = c * 128 + xt * 32 + r * 8
+                        for k in range(2):
+                            start = (line * 32 + xt * 8 + zt * 2 + k) * 64 + c * 4 + r
+                            send_rows[pl.ds(start, 8, stride=8), :] = plane_out[at : at + 8, k * 128 : k * 128 + 128]
+            if order == 0:
 
                 @pl.when(n > 0)
                 def _():
-                    send_first((z + n - 1) % 4, n == 1)
+                    send_first(line, far_first(n - 1), False)
 
             return carry
 
         lax.fori_loop(0, 4, step, 0)
-        if i == 0:
-            send_first((z + 3) % 4, False)
+        if order == 0:
+            send_first(line, far_first(3), True)
+        elif order < 3:
+            send_line(order, line, pl.ds(0, 8), a_sem.at[order])
 
     loads[2].wait()
-    for i in range(2):
-        for step in range(1, 4):
+    other = 1 - yh
+    lines = ((yh, 0), (yh, 1), (other, 0), (other, 1))
+    for order, (row, i) in enumerate(lines):
+        for step in ((2,) if order < 2 else (1, 3)):
             ring_copy(i, step).wait_recv()
-        over_slabs(i)
-        forward_zy(i)
-
+        over_slabs(row, i)
+        forward_zy(order, row * 2 + i)
+
+    last = other * 2 + 1
     for chunk in range(CHUNKS):
-        span = pl.ds(chunk * PAIR_STEP, PAIR_STEP)
-        pltpu.make_async_copy(send.at[1, me, span], recv.at[span, my_second], a_sem.at[chunk]).start()
-
-        def exchange(step, carry):
-            peer = partner(step)
-            pltpu.make_async_remote_copy(
-                send.at[1, peer, span], recv.at[span, my_second], a_out.at[1], a_sem.at[chunk],
-                device_id=plane(peer), device_id_type=MESH,
-            ).start()
-            return carry
-
-        lax.fori_loop(1, 32, exchange, 0)
+        send_line(3, last, pl.ds(chunk * QUADS, QUADS), a_sem.at[3 + chunk])
 
     loads[3].wait()
     loads[4].wait()
     loads[5].wait()
     green_rows = g.reshape(256 * 32, 128)
-    recv_rows = recv.reshape(16 * 512, 128)
-    back_rows = back.reshape(16 * 512, 128)
-
-    def give_back(i, span):
-        mine = pl.ds(pl.multiple_of(i * 256 + me * 8, 8), 8)
-        pltpu.make_async_copy(back.at[span, mine], home.at[i, me, span], h_sem.at[i]).start()
+    recv_rows = recv.reshape(8 * 1024, 128)
+    back_rows = back.reshape(8 * 1024, 128)
+
+    def give_back(slot, lines_of, span):
+        pltpu.make_async_copy(back.at[span, lines_of, mine], home.at[me, span, lines_of], h_sem.at[slot]).start()
 
         def step(n, carry):
             peer = partner(n)
             pltpu.make_async_remote_copy(
-                back.at[span, pl.ds(pl.multiple_of(i * 256 + peer * 8, 8), 8)], home.at[i, me, span],
-                h_out.at[i], h_sem.at[i], device_id=plane(peer), device_id_type=MESH,
+                back.at[span, lines_of, pl.ds(pl.multiple_of(peer * 8, 8), 8)], home.at[me, span, lines_of],
+                h_out.at[slot], h_sem.at[slot], device_id=plane(peer), device_id_type=MESH,
             ).start()
             return carry
 
         lax.fori_loop(1, 32, step, 0)
 
-    whole = recv.at[:, pl.ds(0, 256)]
-    pltpu.make_async_copy(whole, whole, a_sem.at[CHUNKS]).wait()
+    for order, (row, i) in enumerate(lines[:3]):
+        whole = recv.at[:, row * 2 + i]
+        pltpu.make_async_copy(whole, whole, a_sem.at[order]).wait()
     for chunk in range(CHUNKS):
-        span = pl.ds(chunk * PAIR_STEP, PAIR_STEP)
-        arrived = recv.at[span, pl.ds(256, 256)]
-        pltpu.make_async_copy(arrived, arrived, a_sem.at[chunk]).wait()
+        span = pl.ds(chunk * QUADS, QUADS)
+        arrived = recv.at[span, last]
+        pltpu.make_async_copy(arrived, arrived, a_sem.at[3 + chunk]).wait()
 
         def solve(n, carry):
-            pair = chunk * PAIR_STEP + n
-            field = jnp.concatenate([recv_rows[pl.ds(pair * 512 + odd, 256, stride=2), :] for odd in range(2)], 1)
+            quad = chunk * QUADS + n // 2
+            r = 2 * (n % 2)
+            field = jnp.concatenate([recv_rows[pl.ds(quad * 1024 + r + odd, 256, stride=4), :] for odd in range(2)], 1)
             full = dot_nn(weight3(wx[0], wx[1]), data3(field, 0))
-            factor = jnp.concatenate([green_rows[pl.ds(2 * pair + odd, 256, stride=32), :] for odd in range(2)], 1)
+            factor = jnp.concatenate([green_rows[pl.ds(4 * quad + r + odd, 256, stride=32), :] for odd in range(2)], 1)
             product = jnp.concatenate([full[:256] * factor, full[256:] * factor], 0)
             result = dot_nn(weight3(wxi[0], wxi[1]), data3(product, 0))
             for odd in range(2):
-                back_rows[pl.ds(pair * 512 + odd, 256, stride=2), :] = result[:, odd * 128 : odd * 128 + 128]
-            return carry
-
-        lax.fori_loop(0, PAIR_STEP, solve, 0)
-        give_back(0, span)
-    give_back(1, pl.ds(0, 16))
+                back_rows[pl.ds(quad * 1024 + r + odd, 256, stride=4), :] = result[:, odd * 128 : odd * 128 + 128]
+            return carry
+
+        lax.fori_loop(0, 2 * QUADS, solve, 0)
+        give_back(0, pl.ds(other * 2, 2), span)
+    for i in range(2):
+        give_back(1 + i, pl.ds(yh * 2 + i, 1), pl.ds(0, 8))
 
     loads[6].wait()
 
-    def inverse_yz(i):
+    def inverse_yz(line):
         def step(zt, carry):
-            pieces = []
-            for row in range(2):
-                columns = []
-                for k in range(2):
-                    blocks = []
-                    for c in range(2):
-                        for xt in range(4):
-                            for odd in range(2):
-                                start = (i * 32 + xt * 8 + zt * 2 + k) * 128 + c * 4 + row * 2 + odd
-                                blocks.append(home_rows[pl.ds(start, 16, stride=8), :])
-                    columns.append(jnp.concatenate(blocks, 0))
-                along = dot_nn(weight3(wyi[0], wyi[1]), data3(jnp.concatenate(columns, 1), 0))
-                pieces.append(
-                    jnp.concatenate([along[c * 128 : c * 128 + 128, k * 128 : k * 128 + 128] for k in range(2) for c in range(2)], 1)
-                )
-            b[zt] = dot_nt(weight3(wzi[zt, 0], wzi[zt, 1]), data3(jnp.concatenate(pieces, 0), 1))
+            columns = []
+            for k in range(2):
+                blocks = []
+                for c in range(2):
+                    for xt in range(4):
+                        for r in range(4):
+                            start = (xt * 8 + zt * 2 + k) * 256 + line * 8 + c * 4 + r
+                            blocks.append(home_rows[pl.ds(start, 8, stride=32), :])
+                columns.append(jnp.concatenate(blocks, 0))
+            along = dot_nn(weight3(wyi[0], wyi[1]), data3(jnp.concatenate(columns, 1), 0))
+            field = jnp.concatenate(
+                [along[c * 128 : c * 128 + 128, k * 128 : k * 128 + 128] for k in range(2) for c in range(2)], 1
+            )
+            b[zt] = dot_nt(weight3(wzi[zt, 0], wzi[zt, 1]), data3(field, 1))
             return carry
 
         lax.fori_loop(0, 4, step, 0)
 
     def back_to_slabs(i, row):
-        for lanes in (pl.ds(pl.multiple_of(row * 128, 128), 128),):
+        for _ in range(1):
 
             def step(n, carry):
                 at = n * 8
                 turned = []
                 for e in range(2):
                     value = [
-                        [b[slots[j], pl.ds(pl.multiple_of(e * 256 + c * 128 + at, 8), 8), lanes] for c in range(2)]
+                        [b[slots[j], pl.ds(pl.multiple_of(e * 256 + c * 128 + at, 8), 8), :] for c in range(2)]
                         for j in range(4)
                     ]
                     (ar, ai), (br, bi), (cr, ci), (dr, di) = [
@@ -421,16 +428,9 @@
             device_id=ring(member), device_id_type=MESH,
         )
 
-    other = 1 - yh
-
-    def home_half(i):
-        pltpu.make_async_copy(home.at[i], home.at[i], h_sem.at[i]).wait()
-        inverse_yz(i)
-        back_to_slabs(i, other)
-        sum_copy(i, other).start()
-        sum_copy(i, 2 + other).start()
-        back_to_slabs(i, yh)
-        sum_copy(i, (1 - yl) * 2 + yh).start()
+    def home_line(row, i):
+        inverse_yz(row * 2 + i)
+        back_to_slabs(i, row)
 
     def finish(i):
         for step in range(3):
@@ -453,10 +453,18 @@
 
         lax.fori_loop(1, 8, return_slab, 0)
 
-    home_half(0)
-    finish(0)
-    home_half(1)
-    finish(1)
+    both = home.at[:, :, pl.ds(other * 2, 2)]
+    pltpu.make_async_copy(both, both, h_sem.at[0]).wait()
+    for i in range(2):
+        home_line(other, i)
+        sum_copy(i, other).start()
+        sum_copy(i, 2 + other).start()
+    for i in range(2):
+        single = home.at[:, :, yh * 2 + i]
+        pltpu.make_async_copy(single, single, h_sem.at[1 + i]).wait()
+        home_line(yh, i)
+        sum_copy(i, (1 - yl) * 2 + yh).start()
+        finish(i)
     out_rows = out.reshape(64 * 16, 128)
     for i in range(2):
         pltpu.make_async_copy(final.at[:, i], final.at[:, i], f_sem.at[i]).wait()
@@ -469,9 +477,11 @@
     drain(zs.at[pl.ds(0, 14)], z_out)
     for i in range(2):
         drain(raw.at[pl.ds(0, 3), i], y_out.at[i])
-    for i in range(2):
-        drain(send.at[i, pl.ds(0, 31)], a_out.at[i])
-        drain(send.at[i, pl.ds(0, 31)], h_out.at[i])
+    for order in range(4):
+        drain(send.at[order, pl.ds(0, 31)], a_out.at[order])
+    drain(home.at[pl.ds(0, 31), :, pl.ds(0, 2)], h_out.at[0])
+    for i in range(2):
+        drain(home.at[pl.ds(0, 31), :, i], h_out.at[1 + i])
         drain(partial.at[:, i], r_out.at[i])
         drain(final.at[pl.ds(0, 7), i], f_out.at[i])
 
@@ -497,12 +507,12 @@
             pltpu.VMEM((4, 2, 512, 512), BF16),
             pltpu.VMEM((16, 64, 128), F32),
             pltpu.VMEM((4, 2, 4, 128, 128), F32),
-            pltpu.VMEM((4, 2, 2, 256, 256), BF16),
-            pltpu.VMEM((2, 32, 16, 8, 128), F32),
-            pltpu.VMEM((16, 512, 128), F32),
-            pltpu.VMEM((16, 512, 128), F32),
-            pltpu.VMEM((2, 32, 16, 8, 128), F32),
-            pltpu.VMEM((4, 512, 256), F32),
+            pltpu.VMEM((4, 2, 2, 256, 128), BF16),
+            pltpu.VMEM((4, 32, 8, 8, 128), F32),
+            pltpu.VMEM((8, 4, 256, 128), F32),
+            pltpu.VMEM((8, 4, 256, 128), F32),
+            pltpu.VMEM((32, 8, 4, 8, 128), F32),
+            pltpu.VMEM((4, 512, 128), F32),
             pltpu.VMEM((2, 2, 2, 4, 128, 128), F32),
             pltpu.VMEM((3, 2, 4, 128, 128), F32),
             pltpu.VMEM((4, 2, 128, 128), F32),
@@ -512,10 +522,10 @@
             dma,
             dma((2, 3)),
             dma((2,)),
-            dma((CHUNKS + 1,)),
-            dma((2,)),
-            dma((2,)),
-            dma((2,)),
+            dma((3 + CHUNKS,)),
+            dma((4,)),
+            dma((3,)),
+            dma((3,)),
             dma((2, 3)),
             dma((2,)),
             dma((2,)),

time: 165 us -> 151 us (0.915)
  Pallas kernels: 161 us -> 149 us
    pallas_call x1, Pallas kernels: 161 us -> 149 us  [on_device(): pl.pallas_call(kernel, out_shape=jax.ShapeDtypeStruct((64, 16, 128), F32)...]
where the time goes in v2:
time: 151 us
  Pallas kernels  149 us (99%)
  local copies, waits for them, and re-layouts  1.87 us (1%)
    pallas_call x1, Pallas kernels, on_device(): pl.pallas_call(kernel, out_shape=jax.ShapeDtypeStruct((64, 16, 128), F32)...  149 us

profile of v2, /device:TPU:1, one launch (start us, length us, event | category | flops | bytes accessed | tf_op | source)
XLA Modules:
  0.0 150.8 jit_solution(7144313105374947023)
XLA Ops:
  0.0 148.9 %shard_map.82 = f32[64,16,128]{2,1,0:T(8,128)} custom-call(f32[64,16,128]{2,1,0:T(8,128)} %charge.1, f32[256,32,128]{2,1,0:T(8,128)} %green.1, bf16[2,512,256]{2,1,0:T(8,128)(2,1)} %constant.12.clone.wx_hbm, bf16[2,256,512]{2,1,0:T(8,128)(2,1)} %constant.13.clone.wxi_hbm, bf16[2,2,256,256]{3,2,1,0:T(8,128)(2,1)} %constant.14.clone.wy_hbm, ...), custom_call_target="tpu_custom_call" | custom-call | tf_op jit(solution)/shard_map/pallas_call | solution.py:493
  148.9 1.9 %copy.10 = f32[64,16,128]{2,1,0:T(8,128)} copy(f32[64,16,128]{2,1,0:T(8,128)} %shard_map.82) | data formatting | bytes 1048576

commit v3 on v2

--- a/solution.py
+++ b/solution.py
@@ -12,8 +12,7 @@
 MESH = pl.DeviceIdType.MESH
 F32 = jnp.float32
 BF16 = jnp.bfloat16
-CHUNKS = 4
-QUADS = 8 // CHUNKS
+SHARES = ((0, 3), (3, 2), (5, 2), (7, 1))
 
 
 def halves(table):
@@ -83,7 +82,7 @@
     charge, green, wx_hbm, wxi_hbm, wy_hbm, wyi_hbm, alpha_hbm, beta_hbm,
     out,
     g, wx, wxi, wy, wyi, alpha, beta, wz, wzi, zs, raw, a, send, recv, back, home, b, part, partial, total, final,
-    load_sem, z_sem, z_out, y_sem, y_out, a_sem, a_out, h_sem, h_out, r_sem, r_out, f_sem, f_out,
+    load_sem, z_sem, z_out, y_sem, y_out, a_sem, a_out, h_sem, h_out, r_sem, r_out, f_sem, f_out, extra, x_sem, x_out,
 ):
     gz = lax.axis_index("gz")
     ta = lax.axis_index("ta")
@@ -98,6 +97,9 @@
 
     def ring(member):
         return ((member // 2) * 8 + q, (member % 2) * 4 + xc)
+
+    def across(peer):
+        return ((1 - yl) * 8 + peer, ta)
 
     loads = [
         pltpu.make_async_copy(alpha_hbm, alpha, load_sem.at[0]),
@@ -120,16 +122,34 @@
     lax.fori_loop(1, 32, greet, 0)
     for step in range(1, 4):
         pl.semaphore_signal(barrier, inc=1, device_id=ring((ym + step) % 4), device_id_type=MESH)
+
+    def greet_across(step, carry):
+        pl.semaphore_signal(barrier, inc=1, device_id=across((q + step) % 8), device_id_type=MESH)
+        return carry
+
+    lax.fori_loop(1, 8, greet_across, 0)
     rows = charge.reshape(64 * 16, 128)
     for x in range(16):
         zs[x] = rows[pl.ds(x, 64, stride=16), :]
-    pl.semaphore_wait(barrier, 34)
+    pl.semaphore_wait(barrier, 41)
 
     for i in range(2):
         keep = pltpu.make_async_copy(
             zs.at[2 * q + i], raw.at[ym, i, z, pl.ds(core * 64, 64)], z_sem.at[i]
         )
         keep.start()
+
+        if i == 0:
+
+            def spread_across(step, carry):
+                peer = (q + step) % 8
+                pltpu.make_async_remote_copy(
+                    zs.at[2 * peer], raw.at[ym, 0, z, pl.ds(core * 64, 64)], y_out.at[0], y_sem.at[0, 1],
+                    device_id=across(peer), device_id_type=MESH,
+                ).start()
+                return carry
+
+            lax.fori_loop(0, 8, spread_across, 0)
 
         def spread(step, carry):
             peer = (q + step) % 8
@@ -158,14 +178,9 @@
         high, low = split(table)
         wz[slot, 0] = high
         wz[slot, 1] = low
-        odd = (slot % 2).astype(F32)
-        wide = jnp.concatenate(
-            [piece for block in blocks for piece in (block * (1.0 - odd), block * odd)], 0
-        )
-        high, low = split(wide.T)
-        half = pl.multiple_of((slot % 2) * 256, 256)
-        wzi[slot // 2, 0, pl.ds(half, 256), :] = high
-        wzi[slot // 2, 1, pl.ds(half, 256), :] = low
+        high, low = split(table.T)
+        wzi[slot, 0] = high
+        wzi[slot, 1] = low
         return carry
 
     lax.fori_loop(0, 8, build, 0)
@@ -178,7 +193,8 @@
 
     for i in range(2):
         pltpu.make_async_copy(raw.at[ym, i], raw.at[ym, i], z_sem.at[i]).wait()
-        ring_copy(i, 2).start()
+        if i == 1:
+            ring_copy(i, 2).start()
     for i in range(2):
         for step in (1, 3):
             ring_copy(i, step).start()
@@ -299,17 +315,12 @@
                             start = (line * 32 + xt * 8 + zt * 2 + k) * 64 + c * 4 + r
                             send_rows[pl.ds(start, 8, stride=8), :] = plane_out[at : at + 8, k * 128 : k * 128 + 128]
             if order == 0:
-
-                @pl.when(n > 0)
-                def _():
-                    send_first(line, far_first(n - 1), False)
+                send_first(line, zt, n == 3)
 
             return carry
 
         lax.fori_loop(0, 4, step, 0)
-        if order == 0:
-            send_first(line, far_first(3), True)
-        elif order < 3:
+        if 0 < order < 3:
             send_line(order, line, pl.ds(0, 8), a_sem.at[order])
 
     loads[2].wait()
@@ -317,13 +328,14 @@
     lines = ((yh, 0), (yh, 1), (other, 0), (other, 1))
     for order, (row, i) in enumerate(lines):
         for step in ((2,) if order < 2 else (1, 3)):
-            ring_copy(i, step).wait_recv()
+            source = (ym - step) % 4
+            pltpu.make_async_copy(raw.at[source, i], raw.at[source, i], y_sem.at[i, step - 1]).wait()
         over_slabs(row, i)
         forward_zy(order, row * 2 + i)
 
     last = other * 2 + 1
-    for chunk in range(CHUNKS):
-        send_line(3, last, pl.ds(chunk * QUADS, QUADS), a_sem.at[3 + chunk])
+    for share, (begin, size) in enumerate(SHARES):
+        send_line(3, last, pl.ds(begin, size), a_sem.at[3 + share])
 
     loads[3].wait()
     loads[4].wait()
@@ -348,13 +360,13 @@
     for order, (row, i) in enumerate(lines[:3]):
         whole = recv.at[:, row * 2 + i]
         pltpu.make_async_copy(whole, whole, a_sem.at[order]).wait()
-    for chunk in range(CHUNKS):
-        span = pl.ds(chunk * QUADS, QUADS)
+    for share, (begin, size) in enumerate(SHARES):
+        span = pl.ds(begin, size)
         arrived = recv.at[span, last]
-        pltpu.make_async_copy(arrived, arrived, a_sem.at[3 + chunk]).wait()
+        pltpu.make_async_copy(arrived, arrived, a_sem.at[3 + share]).wait()
 
         def solve(n, carry):
-            quad = chunk * QUADS + n // 2
+            quad = begin + n // 2
             r = 2 * (n % 2)
             field = jnp.concatenate([recv_rows[pl.ds(quad * 1024 + r + odd, 256, stride=4), :] for odd in range(2)], 1)
             full = dot_nn(weight3(wx[0], wx[1]), data3(field, 0))
@@ -365,7 +377,7 @@
                 back_rows[pl.ds(quad * 1024 + r + odd, 256, stride=4), :] = result[:, odd * 128 : odd * 128 + 128]
             return carry
 
-        lax.fori_loop(0, 2 * QUADS, solve, 0)
+        lax.fori_loop(0, 2 * size, solve, 0)
         give_back(0, pl.ds(other * 2, 2), span)
     for i in range(2):
         give_back(1 + i, pl.ds(yh * 2 + i, 1), pl.ds(0, 8))
@@ -384,10 +396,15 @@
                             blocks.append(home_rows[pl.ds(start, 8, stride=32), :])
                 columns.append(jnp.concatenate(blocks, 0))
             along = dot_nn(weight3(wyi[0], wyi[1]), data3(jnp.concatenate(columns, 1), 0))
-            field = jnp.concatenate(
-                [along[c * 128 : c * 128 + 128, k * 128 : k * 128 + 128] for k in range(2) for c in range(2)], 1
-            )
-            b[zt] = dot_nt(weight3(wzi[zt, 0], wzi[zt, 1]), data3(field, 1))
+            lower = lax.broadcasted_iota(jnp.int32, (128, 128), 1) < 64
+            fields = [[], []]
+            for k in range(2):
+                re, im = [along[c * 128 : c * 128 + 128, k * 128 : k * 128 + 128] for c in range(2)]
+                fields[0].append(jnp.where(lower, re, pltpu.roll(im, 64, 1)))
+                fields[1].append(jnp.where(lower, pltpu.roll(re, 64, 1), im))
+            for e in range(2):
+                weight = weight3(wzi[zt * 2 + e, 0], wzi[zt * 2 + e, 1])
+                b[zt, e * 256 : e * 256 + 256, :] = dot_nt(weight, data3(jnp.concatenate(fields[e], 1), 1))
             return carry
 
         lax.fori_loop(0, 4, step, 0)
@@ -433,11 +450,12 @@
         back_to_slabs(i, row)
 
     def finish(i):
-        for step in range(3):
-            pltpu.make_async_copy(partial.at[step, i], partial.at[step, i], r_sem.at[i, step]).wait()
+        for slot in (0, 1, 2) if i == 0 else (0, 2):
+            pltpu.make_async_copy(partial.at[slot, i], partial.at[slot, i], r_sem.at[i, slot]).wait()
 
         def add(k, carry):
-            total[k, i] = (part[yl, yh, i, k] + partial[0, i, k]) + (partial[1, i, k] + partial[2, i, k])
+            value = part[yl, yh, i, k] + partial[0, i, k] + partial[2, i, k]
+            total[k, i] = value + partial[1, i, k] if i == 0 else value
             return carry
 
         lax.fori_loop(0, 4, add, 0)
@@ -453,6 +471,14 @@
 
         lax.fori_loop(1, 8, return_slab, 0)
 
+    def return_across(step, carry):
+        peer = (q + step) % 8
+        pltpu.make_async_remote_copy(
+            part.at[1 - yl, yh, 1, peer // 2, pl.ds((peer % 2) * 64, 64)], extra.at[q], x_out, x_sem,
+            device_id=across(peer), device_id_type=MESH,
+        ).start()
+        return carry
+
     both = home.at[:, :, pl.ds(other * 2, 2)]
     pltpu.make_async_copy(both, both, h_sem.at[0]).wait()
     for i in range(2):
@@ -463,13 +489,18 @@
         single = home.at[:, :, yh * 2 + i]
         pltpu.make_async_copy(single, single, h_sem.at[1 + i]).wait()
         home_line(yh, i)
-        sum_copy(i, (1 - yl) * 2 + yh).start()
+        if i == 0:
+            sum_copy(i, (1 - yl) * 2 + yh).start()
+        else:
+            lax.fori_loop(0, 8, return_across, 0)
         finish(i)
     out_rows = out.reshape(64 * 16, 128)
     for i in range(2):
         pltpu.make_async_copy(final.at[:, i], final.at[:, i], f_sem.at[i]).wait()
+        if i == 1:
+            pltpu.make_async_copy(extra, extra, x_sem).wait()
         for n in range(8):
-            out_rows[pl.ds(2 * n + i, 64, stride=16), :] = final[n, i]
+            out_rows[pl.ds(2 * n + i, 64, stride=16), :] = final[n, i] + extra[n] if i else final[n, i]
 
     def drain(ref, sem):
         pltpu.make_async_copy(ref, ref, sem).wait()
@@ -482,8 +513,9 @@
     drain(home.at[pl.ds(0, 31), :, pl.ds(0, 2)], h_out.at[0])
     for i in range(2):
         drain(home.at[pl.ds(0, 31), :, i], h_out.at[1 + i])
-        drain(partial.at[:, i], r_out.at[i])
+        drain(partial.at[pl.ds(0, 3 - i), i], r_out.at[i])
         drain(final.at[pl.ds(0, 7), i], f_out.at[i])
+    drain(extra, x_out)
 
 
 def on_device(consts, charge, green_hat):
@@ -504,7 +536,7 @@
             pltpu.VMEM((2, 128, 128), F32),
             pltpu.VMEM((8, 8, 128), F32),
             pltpu.VMEM((8, 2, 256, 256), BF16),
-            pltpu.VMEM((4, 2, 512, 512), BF16),
+            pltpu.VMEM((8, 2, 256, 256), BF16),
             pltpu.VMEM((16, 64, 128), F32),
             pltpu.VMEM((4, 2, 4, 128, 128), F32),
             pltpu.VMEM((4, 2, 2, 256, 128), BF16),
@@ -522,7 +554,7 @@
             dma,
             dma((2, 3)),
             dma((2,)),
-            dma((3 + CHUNKS,)),
+            dma((3 + len(SHARES),)),
             dma((4,)),
             dma((3,)),
             dma((3,)),
@@ -530,6 +562,9 @@
             dma((2,)),
             dma((2,)),
             dma((2,)),
+            pltpu.VMEM((8, 64, 128), F32),
+            dma,
+            dma,
         ],
         compiler_params=pltpu.CompilerParams(
             collective_id=0, has_side_effects=True, vmem_limit_bytes=60 * 1024 * 1024

time: 151 us -> 144 us (0.954)
  Pallas kernels: 149 us -> 142 us
    pallas_call x1, Pallas kernels: 149 us -> 142 us  [on_device(): pl.pallas_call(kernel, out_shape=jax.ShapeDtypeStruct((64, 16, 128), F32)...]
where the time goes in v3:
time: 144 us
  Pallas kernels  142 us (99%)
  local copies, waits for them, and re-layouts  1.87 us (1%)
    pallas_call x1, Pallas kernels, on_device(): pl.pallas_call(kernel, out_shape=jax.ShapeDtypeStruct((64, 16, 128), F32)...  142 us

profile of v3, /device:TPU:1, one launch (start us, length us, event | category | flops | bytes accessed | tf_op | source)
XLA Modules:
  0.0 143.6 jit_solution(11261176892423900179)
XLA Ops:
  0.0 141.7 %shard_map.82 = f32[64,16,128]{2,1,0:T(8,128)} custom-call(f32[64,16,128]{2,1,0:T(8,128)} %charge.1, f32[256,32,128]{2,1,0:T(8,128)} %green.1, bf16[2,512,256]{2,1,0:T(8,128)(2,1)} %constant.12.clone.wx_hbm, bf16[2,256,512]{2,1,0:T(8,128)(2,1)} %constant.13.clone.wxi_hbm, bf16[2,2,256,256]{3,2,1,0:T(8,128)(2,1)} %constant.14.clone.wy_hbm, ...), custom_call_target="tpu_custom_call" | custom-call | tf_op jit(solution)/shard_map/pallas_call | solution.py:525
  141.7 1.9 %copy.10 = f32[64,16,128]{2,1,0:T(8,128)} copy(f32[64,16,128]{2,1,0:T(8,128)} %shard_map.82) | data formatting | bytes 1048576

commit v4 on v3

--- a/solution.py
+++ b/solution.py
@@ -12,7 +12,7 @@
 MESH = pl.DeviceIdType.MESH
 F32 = jnp.float32
 BF16 = jnp.bfloat16
-SHARES = ((0, 3), (3, 2), (5, 2), (7, 1))
+SHARES = ((0, 3), (3, 3), (6, 2))
 
 
 def halves(table):
@@ -86,17 +86,17 @@
 ):
     gz = lax.axis_index("gz")
     ta = lax.axis_index("ta")
-    yl, q = gz // 8, gz % 8
-    z, core = q // 2, q % 2
-    yh, xc = ta // 4, ta % 4
+    yl, q = gz >> 3, gz & 7
+    z, core = q >> 1, q & 1
+    yh, xc = ta >> 2, ta & 3
     ym = yl * 2 + yh
     me = xc * 8 + q
 
     def plane(peer):
-        return (yl * 8 + peer % 8, yh * 4 + peer // 8)
+        return (yl * 8 + (peer & 7), yh * 4 + (peer >> 3))
 
     def ring(member):
-        return ((member // 2) * 8 + q, (member % 2) * 4 + xc)
+        return ((member >> 1) * 8 + q, (member & 1) * 4 + xc)
 
     def across(peer):
         return ((1 - yl) * 8 + peer, ta)
@@ -116,15 +116,15 @@
     barrier = pltpu.get_barrier_semaphore()
 
     def greet(step, carry):
-        pl.semaphore_signal(barrier, inc=1, device_id=plane((me + step) % 32), device_id_type=MESH)
+        pl.semaphore_signal(barrier, inc=1, device_id=plane((me + step) & 31), device_id_type=MESH)
         return carry
 
     lax.fori_loop(1, 32, greet, 0)
     for step in range(1, 4):
-        pl.semaphore_signal(barrier, inc=1, device_id=ring((ym + step) % 4), device_id_type=MESH)
+        pl.semaphore_signal(barrier, inc=1, device_id=ring((ym + step) & 3), device_id_type=MESH)
 
     def greet_across(step, carry):
-        pl.semaphore_signal(barrier, inc=1, device_id=across((q + step) % 8), device_id_type=MESH)
+        pl.semaphore_signal(barrier, inc=1, device_id=across((q + step) & 7), device_id_type=MESH)
         return carry
 
     lax.fori_loop(1, 8, greet_across, 0)
@@ -142,7 +142,7 @@
         if i == 0:
 
             def spread_across(step, carry):
-                peer = (q + step) % 8
+                peer = (q + step) & 7
                 pltpu.make_async_remote_copy(
                     zs.at[2 * peer], raw.at[ym, 0, z, pl.ds(core * 64, 64)], y_out.at[0], y_sem.at[0, 1],
                     device_id=across(peer), device_id_type=MESH,
@@ -152,7 +152,7 @@
             lax.fori_loop(0, 8, spread_across, 0)
 
         def spread(step, carry):
-            peer = (q + step) % 8
+            peer = (q + step) & 7
             pltpu.make_async_remote_copy(
                 zs.at[2 * peer + i], raw.at[ym, i, z, pl.ds(core * 64, 64)], z_out, z_sem.at[i],
                 device_id=(yl * 8 + peer, ta), device_id_type=MESH,
@@ -188,7 +188,7 @@
     def ring_copy(i, step):
         return pltpu.make_async_remote_copy(
             raw.at[ym, i], raw.at[ym, i], y_out.at[i], y_sem.at[i, step - 1],
-            device_id=ring((ym + step) % 4), device_id_type=MESH,
+            device_id=ring((ym + step) & 3), device_id_type=MESH,
         )
 
     for i in range(2):
@@ -243,56 +243,32 @@
 
             lax.fori_loop(0, 8, step, 0)
 
-    send_rows = send.reshape(4 * 32 * 64, 128)
+    send_rows = send.reshape(32 * 256, 128)
     home_rows = home.reshape(32 * 256, 128)
     mine = pl.ds(pl.multiple_of(me * 8, 8), 8)
 
     def partner(step):
-        turn = step // 2
-        return ((xc + turn) % 4) * 8 + ((z + turn // 4 + turn) % 4) * 2 + (core + step) % 2
-
-
-    def plane_copy(line, peer, span, slot, sem):
-        return pltpu.make_async_remote_copy(
-            send.at[line, peer, span], recv.at[span, line, mine], a_out.at[slot], sem,
-            device_id=plane(peer), device_id_type=MESH,
-        )
-
-    def plane_keep(line, span, sem):
-        pltpu.make_async_copy(send.at[line, me, span], recv.at[span, line, mine], sem).start()
-
-    def send_first(line, zt, here):
+        turn = step >> 1
+        xt = (xc + turn) & 3
+        zc = (((z + (turn >> 2) + turn) & 3) << 1) + ((core + step) & 1)
+        return (xt << 3) + zc, (yl * 8 + zc, yh * 4 + xt)
+
+    def send_lines(lines_of, span, out_sem, sem):
+        pltpu.make_async_copy(send.at[me, span, lines_of], recv.at[span, lines_of, mine], sem).start()
+
         def step(n, carry):
-            peer = ((xc + n // 2) % 4) * 8 + zt * 2 + (core + n) % 2
-            keep = jnp.logical_and(here, n == 0)
-
-            @pl.when(keep)
-            def _():
-                plane_keep(line, pl.ds(0, 8), a_sem.at[0])
-
-            @pl.when(jnp.logical_not(keep))
-            def _():
-                plane_copy(line, peer, pl.ds(0, 8), 0, a_sem.at[0]).start()
-
-            return carry
-
-        lax.fori_loop(0, 8, step, 0)
-
-    def send_line(order, line, span, sem):
-        plane_keep(line, span, sem)
-
-        def step(n, carry):
-            plane_copy(line, partner(n), span, order, sem).start()
+            peer, place = partner(n)
+            pltpu.make_async_remote_copy(
+                send.at[peer, span, lines_of], recv.at[span, lines_of, mine], out_sem, sem,
+                device_id=place, device_id_type=MESH,
+            ).start()
             return carry
 
         lax.fori_loop(1, 32, step, 0)
-
-    def far_first(n):
-        return (z + jnp.where(n == 0, 2, jnp.where(n == 1, 1, jnp.where(n == 2, 3, 0)))) % 4
 
     def forward_zy(order, line):
         def step(n, carry):
-            zt = far_first(n)
+            zt = n
             outs = []
             for e in range(2):
                 weight = weight3(wz[zt * 2 + e, 0], wz[zt * 2 + e, 1])
@@ -312,30 +288,29 @@
                     for r in range(4):
                         at = c * 128 + xt * 32 + r * 8
                         for k in range(2):
-                            start = (line * 32 + xt * 8 + zt * 2 + k) * 64 + c * 4 + r
-                            send_rows[pl.ds(start, 8, stride=8), :] = plane_out[at : at + 8, k * 128 : k * 128 + 128]
-            if order == 0:
-                send_first(line, zt, n == 3)
+                            start = (xt * 8 + zt * 2 + k) * 256 + line * 8 + c * 4 + r
+                            send_rows[pl.ds(start, 8, stride=32), :] = plane_out[at : at + 8, k * 128 : k * 128 + 128]
 
             return carry
 
         lax.fori_loop(0, 4, step, 0)
-        if 0 < order < 3:
-            send_line(order, line, pl.ds(0, 8), a_sem.at[order])
+        if order < 2:
+            for begin in (0, 4):
+                send_lines(pl.ds(line, 1), pl.ds(begin, 4), a_out.at[order], a_sem.at[order])
 
     loads[2].wait()
     other = 1 - yh
     lines = ((yh, 0), (yh, 1), (other, 0), (other, 1))
     for order, (row, i) in enumerate(lines):
         for step in ((2,) if order < 2 else (1, 3)):
-            source = (ym - step) % 4
+            source = (ym - step) & 3
             pltpu.make_async_copy(raw.at[source, i], raw.at[source, i], y_sem.at[i, step - 1]).wait()
         over_slabs(row, i)
         forward_zy(order, row * 2 + i)
 
-    last = other * 2 + 1
+    late = pl.ds(other * 2, 2)
     for share, (begin, size) in enumerate(SHARES):
-        send_line(3, last, pl.ds(begin, size), a_sem.at[3 + share])
+        send_lines(late, pl.ds(begin, size), a_out.at[2], a_sem.at[2 + share])
 
     loads[3].wait()
     loads[4].wait()
@@ -348,22 +323,22 @@
         pltpu.make_async_copy(back.at[span, lines_of, mine], home.at[me, span, lines_of], h_sem.at[slot]).start()
 
         def step(n, carry):
-            peer = partner(n)
+            peer, place = partner(n)
             pltpu.make_async_remote_copy(
                 back.at[span, lines_of, pl.ds(pl.multiple_of(peer * 8, 8), 8)], home.at[me, span, lines_of],
-                h_out.at[slot], h_sem.at[slot], device_id=plane(peer), device_id_type=MESH,
+                h_out.at[slot], h_sem.at[slot], device_id=place, device_id_type=MESH,
             ).start()
             return carry
 
         lax.fori_loop(1, 32, step, 0)
 
-    for order, (row, i) in enumerate(lines[:3]):
+    for order, (row, i) in enumerate(lines[:2]):
         whole = recv.at[:, row * 2 + i]
         pltpu.make_async_copy(whole, whole, a_sem.at[order]).wait()
     for share, (begin, size) in enumerate(SHARES):
         span = pl.ds(begin, size)
-        arrived = recv.at[span, last]
-        pltpu.make_async_copy(arrived, arrived, a_sem.at[3 + share]).wait()
+        arrived = recv.at[span, late]
+        pltpu.make_async_copy(arrived, arrived, a_sem.at[2 + share]).wait()
 
         def solve(n, carry):
             quad = begin + n // 2
@@ -439,9 +414,9 @@
             lax.fori_loop(0, 16, step, 0)
 
     def sum_copy(i, member):
-        slot = (ym - member) % 4 - 1
+        slot = ((ym - member) & 3) - 1
         return pltpu.make_async_remote_copy(
-            part.at[member // 2, member % 2, i], partial.at[slot, i], r_out.at[i], r_sem.at[i, slot],
+            part.at[member >> 1, member & 1, i], partial.at[slot, i], r_out.at[i], r_sem.at[i, slot],
             device_id=ring(member), device_id_type=MESH,
         )
 
@@ -462,9 +437,9 @@
         pltpu.make_async_copy(total.at[z, i, pl.ds(core * 64, 64)], final.at[q, i], f_sem.at[i]).start()
 
         def return_slab(step, carry):
-            peer = (q + step) % 8
+            peer = (q + step) & 7
             pltpu.make_async_remote_copy(
-                total.at[peer // 2, i, pl.ds((peer % 2) * 64, 64)], final.at[q, i], f_out.at[i], f_sem.at[i],
+                total.at[peer >> 1, i, pl.ds((peer & 1) * 64, 64)], final.at[q, i], f_out.at[i], f_sem.at[i],
                 device_id=(yl * 8 + peer, ta), device_id_type=MESH,
             ).start()
             return carry
@@ -472,9 +447,9 @@
         lax.fori_loop(1, 8, return_slab, 0)
 
     def return_across(step, carry):
-        peer = (q + step) % 8
+        peer = (q + step) & 7
         pltpu.make_async_remote_copy(
-            part.at[1 - yl, yh, 1, peer // 2, pl.ds((peer % 2) * 64, 64)], extra.at[q], x_out, x_sem,
+            part.at[1 - yl, yh, 1, peer >> 1, pl.ds((peer & 1) * 64, 64)], extra.at[q], x_out, x_sem,
             device_id=across(peer), device_id_type=MESH,
         ).start()
         return carry
@@ -508,8 +483,9 @@
     drain(zs.at[pl.ds(0, 14)], z_out)
     for i in range(2):
         drain(raw.at[pl.ds(0, 3), i], y_out.at[i])
-    for order in range(4):
-        drain(send.at[order, pl.ds(0, 31)], a_out.at[order])
+    for order in range(2):
+        drain(send.at[pl.ds(0, 31), :, order], a_out.at[order])
+    drain(send.at[pl.ds(0, 31), :, pl.ds(0, 2)], a_out.at[2])
     drain(home.at[pl.ds(0, 31), :, pl.ds(0, 2)], h_out.at[0])
     for i in range(2):
         drain(home.at[pl.ds(0, 31), :, i], h_out.at[1 + i])
@@ -540,7 +516,7 @@
             pltpu.VMEM((16, 64, 128), F32),
             pltpu.VMEM((4, 2, 4, 128, 128), F32),
             pltpu.VMEM((4, 2, 2, 256, 128), BF16),
-            pltpu.VMEM((4, 32, 8, 8, 128), F32),
+            pltpu.VMEM((32, 8, 4, 8, 128), F32),
             pltpu.VMEM((8, 4, 256, 128), F32),
             pltpu.VMEM((8, 4, 256, 128), F32),
             pltpu.VMEM((32, 8, 4, 8, 128), F32),
@@ -554,7 +530,7 @@
             dma,
             dma((2, 3)),
             dma((2,)),
-            dma((3 + len(SHARES),)),
+            dma((2 + len(SHARES),)),
             dma((4,)),
             dma((3,)),
             dma((3,)),

time: 144 us -> 138 us (0.958)
  Pallas kernels: 142 us -> 136 us
    pallas_call x1, Pallas kernels: 142 us -> 136 us  [on_device(): pl.pallas_call(kernel, out_shape=jax.ShapeDtypeStruct((64, 16, 128), F32)...]
where the time goes in v4:
time: 138 us; the launch traced here: 137 us
  Pallas kernels  136 us (99%)
  local copies, waits for them, and re-layouts  1.87 us (1%)
    pallas_call x1, Pallas kernels, on_device(): pl.pallas_call(kernel, out_shape=jax.ShapeDtypeStruct((64, 16, 128), F32)...  136 us

profile of v4, /device:TPU:1, one launch (start us, length us, event | category | flops | bytes accessed | tf_op | source)
XLA Modules:
  0.0 137.4 jit_solution(6134543054858374887)
XLA Ops:
  0.0 135.5 %shard_map.82 = f32[64,16,128]{2,1,0:T(8,128)} custom-call(f32[64,16,128]{2,1,0:T(8,128)} %charge.1, f32[256,32,128]{2,1,0:T(8,128)} %green.1, bf16[2,512,256]{2,1,0:T(8,128)(2,1)} %constant.12.clone.wx_hbm, bf16[2,256,512]{2,1,0:T(8,128)(2,1)} %constant.13.clone.wxi_hbm, bf16[2,2,256,256]{3,2,1,0:T(8,128)(2,1)} %constant.14.clone.wy_hbm, ...), custom_call_target="tpu_custom_call" | custom-call | tf_op jit(solution)/shard_map/pallas_call | solution.py:501
  135.5 1.9 %copy.10 = f32[64,16,128]{2,1,0:T(8,128)} copy(f32[64,16,128]{2,1,0:T(8,128)} %shard_map.82) | data formatting | bytes 1048576

commit v5 on v4

--- a/solution.py
+++ b/solution.py
@@ -468,7 +468,8 @@
             sum_copy(i, (1 - yl) * 2 + yh).start()
         else:
             lax.fori_loop(0, 8, return_across, 0)
-        finish(i)
+            finish(0)
+            finish(1)
     out_rows = out.reshape(64 * 16, 128)
     for i in range(2):
         pltpu.make_async_copy(final.at[:, i], final.at[:, i], f_sem.at[i]).wait()

time: 138 us -> 139 us (level)
  no operation moved by 1% of the time
where the time goes in v5:
time: 139 us
  Pallas kernels  137 us (99%)
  local copies, waits for them, and re-layouts  1.87 us (1%)
    pallas_call x1, Pallas kernels, on_device(): pl.pallas_call(kernel, out_shape=jax.ShapeDtypeStruct((64, 16, 128), F32)...  137 us

profile of v5, /device:TPU:1, one launch (start us, length us, event | category | flops | bytes accessed | tf_op | source)
XLA Modules:
  0.0 138.5 jit_solution(7564366053340506237)
XLA Ops:
  0.0 136.7 %shard_map.82 = f32[64,16,128]{2,1,0:T(8,128)} custom-call(f32[64,16,128]{2,1,0:T(8,128)} %charge.1, f32[256,32,128]{2,1,0:T(8,128)} %green.1, bf16[2,512,256]{2,1,0:T(8,128)(2,1)} %constant.12.clone.wx_hbm, bf16[2,256,512]{2,1,0:T(8,128)(2,1)} %constant.13.clone.wxi_hbm, bf16[2,2,256,256]{3,2,1,0:T(8,128)(2,1)} %constant.14.clone.wy_hbm, ...), custom_call_target="tpu_custom_call" | custom-call | tf_op jit(solution)/shard_map/pallas_call | solution.py:502
  136.7 1.9 %copy.10 = f32[64,16,128]{2,1,0:T(8,128)} copy(f32[64,16,128]{2,1,0:T(8,128)} %shard_map.82) | data formatting | bytes 1048576
